TPU v7x, 32 devices: a whole 2x2x4 slice. The times are simulated.
32 devices in a mesh: wide: 8 (over y, x, core), narrow: 4 (over z).
Axes of the slice: x: 2, y: 2, z: 4, core: 2. Of those that a mesh axis runs over, the one named last changes fastest.
Arguments:
- tokens: bfloat16 [32, 512, 256], P('wide', 'narrow'), may hold values from -6 to 6
- kind: int32 [32], P('wide'), may hold values from 0 to 1
- proj_weight: bfloat16 [2, 256, 768], replicated, may hold values from -0.375 to 0.375
- proj_bias: float32 [2, 768], replicated, may hold values from -1.8 to 1.8
- ln1_gain: float32 [768], replicated, may hold values from 0.5 to 1.5
- ln1_bias: float32 [768], replicated, may hold values from -1.2 to 1.2
- qkv_weight: bfloat16 [768, 3, 768], P(None, None, 'narrow'), may hold values from -0.21875 to 0.21875
- qv_bias: float32 [2, 768], P(None, 'narrow'), may hold values from -1.8 to 1.8
- out_weight: bfloat16 [768, 768], P('narrow'), may hold values from -0.75 to 0.75
- out_bias: float32 [768], replicated, may hold values from -1.2 to 1.2
- ln2_gain: float32 [768], replicated, may hold values from 0.5 to 1.5
- ln2_bias: float32 [768], replicated, may hold values from -1.2 to 1.2
- up_weight: bfloat16 [768, 3072], P(None, 'narrow'), may hold values from -0.21875 to 0.21875
- up_bias: float32 [3072], replicated, may hold values from -1.8 to 1.8
- down_weight: bfloat16 [3072, 768], P('narrow'), may hold values from -0.109375 to 0.109375
- down_bias: float32 [768], replicated, may hold values from -1.2 to 1.2
- cotangent: bfloat16 [32, 512, 768], P('wide', 'narrow'), may hold values from -6 to 6
Outputs:
- out: bfloat16 [32, 512, 768], P('wide', 'narrow')
- tokens_grad: float32 [32, 512, 256], P('wide', 'narrow')
- proj_weight_grad: float32 [2, 256, 768], replicated
- proj_bias_grad: float32 [2, 768], replicated
- ln1_gain_grad: float32 [768], replicated
- ln1_bias_grad: float32 [768], replicated
- qkv_weight_grad: float32 [768, 3, 768], P(None, None, 'narrow')
- qv_bias_grad: float32 [2, 768], P(None, 'narrow')
- out_weight_grad: float32 [768, 768], P('narrow')
- out_bias_grad: float32 [768], replicated
- ln2_gain_grad: float32 [768], replicated
- ln2_bias_grad: float32 [768], replicated
- up_weight_grad: float32 [768, 3072], P(None, 'narrow')
- up_bias_grad: float32 [3072], P('narrow')
- down_weight_grad: float32 [3072, 768], P('narrow')
- down_bias_grad: float32 [768], replicated
Inputs may be any that keep to these rules, and one draw needn't show every extreme that they name: kind[c] is 0 for a clip of frame tokens and 1 for a clip of patch tokens.
All inputs are finite; a program needn't handle non-finite values.
Results may differ from a plain program's by a relative error of at most 0.019.
Values may be sent and summed in bfloat16 or wider, within the bound.
No kernel may reach another device: no remote copies, remote signals or barrier semaphores. Data moves between devices by JAX's collectives and lax.ppermute only.
A program may use at most 192 MiB of HBM per device.

v0:
```python
import jax
import jax.numpy as jnp
from jax import lax
from jax.sharding import PartitionSpec as P

HEAD_DIM = 64


epsilon = 1e-06


def layer_norm(values, norm_gain, norm_shift):
    row_mean = jnp.mean(values, axis=-1, keepdims=True)
    centred = values - row_mean
    row_var = jnp.mean(centred * centred, axis=-1, keepdims=True)
    return centred * lax.rsqrt(row_var + epsilon) * norm_gain + norm_shift


def exact_gelu(values):
    return 0.5 * values * (1.0 + jax.scipy.special.erf(values * 2.0 ** (-0.5)))


def project_heads(rows_full, qkv_weight, qv_bias):
    zero_row = jnp.zeros_like(qv_bias[0])
    bias_three = jnp.stack([qv_bias[0], zero_row, qv_bias[1]])
    projected = jnp.einsum(
        "cld,dke->kcle", rows_full, qkv_weight, preferred_element_type=jnp.float32
    )
    projected = (projected + bias_three[:, None, None, :]).astype(jnp.bfloat16)
    head_count = projected.shape[3] // HEAD_DIM
    return projected.reshape(3, projected.shape[1], projected.shape[2], head_count, HEAD_DIM)


def score_block(heads_qkv):
    return jnp.einsum(
        "clhe,cmhe->chlm", heads_qkv[0], heads_qkv[1], preferred_element_type=jnp.float32
    ) * HEAD_DIM ** (-0.5)


def mix_values(probs_low, heads_qkv):
    mixed = jnp.einsum(
        "chlm,cmhe->clhe", probs_low, heads_qkv[2], preferred_element_type=jnp.float32
    )
    mixed = mixed.astype(jnp.bfloat16)
    return mixed.reshape(mixed.shape[0], mixed.shape[1], mixed.shape[2] * mixed.shape[3])


def ffn_backward(rows_in, grad_rows, weight_in, weight_out, bias_in):
    hidden_pre = (
        jnp.einsum("cld,df->clf", rows_in, weight_in, preferred_element_type=jnp.float32) + bias_in
    )
    hidden_back = exact_gelu(hidden_pre).astype(jnp.bfloat16)
    out_grad = jnp.einsum("clf,cld->fd", hidden_back, grad_rows, preferred_element_type=jnp.float32)
    hidden_grad = jnp.einsum(
        "cld,fd->clf", grad_rows, weight_out, preferred_element_type=jnp.float32
    )
    gelu_value, gelu_pull = jax.vjp(exact_gelu, hidden_pre)
    pre_grad = gelu_pull(hidden_grad)[0].astype(jnp.bfloat16)
    in_grad = jnp.einsum("cld,clf->df", rows_in, pre_grad, preferred_element_type=jnp.float32)
    in_bias_grad = jnp.sum(pre_grad, axis=(0, 1), dtype=jnp.float32)
    rows_grad = jnp.einsum("clf,df->cld", pre_grad, weight_in, preferred_element_type=jnp.float32)
    return (in_grad, in_bias_grad, out_grad, rows_grad)


def per_device(
    tokens,
    kind,
    proj_weight,
    proj_bias,
    ln1_gain,
    ln1_bias,
    qkv_weight,
    qv_bias,
    out_weight,
    out_bias,
    ln2_gain,
    ln2_bias,
    up_weight,
    up_bias,
    down_weight,
    down_bias,
    cotangent,
):
    unit_share = up_weight.shape[1]
    local_bias = lax.dynamic_slice_in_dim(
        up_bias, lax.axis_index("narrow") * unit_share, unit_share, 0
    )
    is_patch = kind == 1
    chosen = jnp.where(is_patch[:, None, None], proj_weight[1], proj_weight[0])
    chosen_bias = jnp.where(is_patch[:, None], proj_bias[1], proj_bias[0])
    start_rows = (
        jnp.einsum("clf,cfd->cld", tokens, chosen, preferred_element_type=jnp.float32)
        + chosen_bias[:, None, :]
    )
    normed_one = layer_norm(start_rows, ln1_gain, ln1_bias).astype(jnp.bfloat16)
    rows_one = lax.all_gather(normed_one, "narrow", axis=1, tiled=True)
    heads_qkv = project_heads(rows_one, qkv_weight, qv_bias)
    scores = score_block(heads_qkv)
    row_max = jnp.max(scores, axis=-1, keepdims=True)
    log_total = row_max + jnp.log(jnp.sum(jnp.exp(scores - row_max), axis=-1, keepdims=True))
    probs_low = jnp.exp(scores - log_total).astype(jnp.bfloat16)
    mixed = mix_values(probs_low, heads_qkv)
    attn_part = jnp.einsum("cle,ed->cld", mixed, out_weight, preferred_element_type=jnp.float32)
    attn_rows = lax.psum_scatter(
        attn_part.astype(jnp.bfloat16), "narrow", scatter_dimension=1, tiled=True
    ).astype(jnp.float32)
    middle = start_rows + attn_rows + out_bias
    normed_two = layer_norm(middle, ln2_gain, ln2_bias).astype(jnp.bfloat16)
    rows_two = lax.all_gather(normed_two, "narrow", axis=1, tiled=True)
    hidden = exact_gelu(
        jnp.einsum("cld,df->clf", rows_two, up_weight, preferred_element_type=jnp.float32)
        + local_bias
    ).astype(jnp.bfloat16)
    mlp_part = jnp.einsum("clf,fd->cld", hidden, down_weight, preferred_element_type=jnp.float32)
    mlp_rows = lax.psum_scatter(
        mlp_part.astype(jnp.bfloat16), "narrow", scatter_dimension=1, tiled=True
    ).astype(jnp.float32)
    final_rows = middle + mlp_rows + down_bias
    output = final_rows.astype(jnp.bfloat16)
    down_bias_grad = jnp.sum(cotangent, axis=(0, 1), dtype=jnp.float32)
    grad_all = lax.all_gather(cotangent, "narrow", axis=1, tiled=True)
    rows_two_back = lax.all_gather(normed_two, "narrow", axis=1, tiled=True)
    up_weight_grad, up_bias_grad, down_weight_grad, norm_two_part = ffn_backward(
        rows_two_back, grad_all, up_weight, down_weight, local_bias
    )
    norm_two_grad = lax.psum_scatter(
        norm_two_part.astype(jnp.bfloat16), "narrow", scatter_dimension=1, tiled=True
    ).astype(jnp.float32)
    ln_value, ln_pull = jax.vjp(layer_norm, middle, ln2_gain, ln2_bias)
    mid_grad, ln2_gain_grad, ln2_bias_grad = ln_pull(norm_two_grad)
    mid_grad = mid_grad + cotangent.astype(jnp.float32)
    mid_low = mid_grad.astype(jnp.bfloat16)
    out_bias_grad = jnp.sum(mid_low, axis=(0, 1), dtype=jnp.float32)
    mid_all = lax.all_gather(mid_low, "narrow", axis=1, tiled=True)
    rows_one_back = lax.all_gather(normed_one, "narrow", axis=1, tiled=True)
    heads_back = project_heads(rows_one_back, qkv_weight, qv_bias)
    probs = jnp.exp(score_block(heads_back) - log_total)
    probs_back = probs.astype(jnp.bfloat16)
    mixed_back = mix_values(probs_back, heads_back)
    out_weight_grad = jnp.einsum(
        "cle,cld->ed", mixed_back, mid_all, preferred_element_type=jnp.float32
    )
    mixed_grad = jnp.einsum("cld,ed->cle", mid_all, out_weight, preferred_element_type=jnp.float32)
    mixed_grad = mixed_grad.astype(jnp.bfloat16).reshape(heads_back.shape[1:])
    probs_grad = jnp.einsum(
        "clhe,cmhe->chlm", mixed_grad, heads_back[2], preferred_element_type=jnp.float32
    )
    value_grad = jnp.einsum(
        "chlm,clhe->cmhe", probs_back, mixed_grad, preferred_element_type=jnp.float32
    )
    score_grad = probs * (probs_grad - jnp.sum(probs * probs_grad, axis=-1, keepdims=True))
    score_grad = score_grad.astype(jnp.bfloat16)
    query_grad = jnp.einsum(
        "chlm,cmhe->clhe", score_grad, heads_back[1], preferred_element_type=jnp.float32
    ) * HEAD_DIM ** (-0.5)
    key_grad = jnp.einsum(
        "chlm,clhe->cmhe", score_grad, heads_back[0], preferred_element_type=jnp.float32
    ) * HEAD_DIM ** (-0.5)
    stacked = jnp.stack([query_grad, key_grad, value_grad]).astype(jnp.bfloat16)
    stacked = stacked.reshape(
        3, stacked.shape[1], stacked.shape[2], stacked.shape[3] * stacked.shape[4]
    )
    qkv_weight_grad = jnp.einsum(
        "cld,kcle->dke", rows_one_back, stacked, preferred_element_type=jnp.float32
    )
    qv_bias_grad = jnp.stack(
        [
            jnp.sum(stacked[0], axis=(0, 1), dtype=jnp.float32),
            jnp.sum(stacked[2], axis=(0, 1), dtype=jnp.float32),
        ]
    )
    norm_one_part = jnp.einsum(
        "kcle,dke->cld", stacked, qkv_weight, preferred_element_type=jnp.float32
    )
    norm_one_grad = lax.psum_scatter(
        norm_one_part.astype(jnp.bfloat16), "narrow", scatter_dimension=1, tiled=True
    ).astype(jnp.float32)
    first_value, first_pull = jax.vjp(layer_norm, start_rows, ln1_gain, ln1_bias)
    start_grad, ln1_gain_grad, ln1_bias_grad = first_pull(norm_one_grad)
    start_low = (start_grad + mid_grad).astype(jnp.bfloat16)
    tokens_grad = jnp.einsum("cld,cfd->clf", start_low, chosen, preferred_element_type=jnp.float32)
    per_clip = jnp.einsum("clf,cld->cfd", tokens, start_low, preferred_element_type=jnp.float32)
    clip_bias = jnp.sum(start_low, axis=1, dtype=jnp.float32)
    proj_weight_grad = jnp.stack(
        [
            jnp.sum(jnp.where(is_patch[:, None, None], 0.0, per_clip), axis=0),
            jnp.sum(jnp.where(is_patch[:, None, None], per_clip, 0.0), axis=0),
        ]
    )
    proj_bias_grad = jnp.stack(
        [
            jnp.sum(jnp.where(is_patch[:, None], 0.0, clip_bias), axis=0),
            jnp.sum(jnp.where(is_patch[:, None], clip_bias, 0.0), axis=0),
        ]
    )
    common = lax.psum(
        (
            proj_weight_grad,
            proj_bias_grad,
            ln1_gain_grad,
            ln1_bias_grad,
            out_bias_grad,
            ln2_gain_grad,
            ln2_bias_grad,
            down_bias_grad,
        ),
        ("wide", "narrow"),
    )
    summed = lax.psum(
        (
            qkv_weight_grad,
            qv_bias_grad,
            out_weight_grad,
            up_weight_grad,
            up_bias_grad,
            down_weight_grad,
        ),
        "wide",
    )
    qkv_sum, qv_sum, out_sum, up_sum, up_bias_sum, down_sum = summed
    return (
        output,
        tokens_grad,
        common[0],
        common[1],
        common[2],
        common[3],
        qkv_sum,
        qv_sum,
        out_sum,
        common[4],
        common[5],
        common[6],
        up_sum,
        up_bias_sum,
        down_sum,
        common[7],
    )


def solution(mesh):
    in_specs = (
        P("wide", "narrow", None),
        P("wide"),
        P(),
        P(),
        P(),
        P(),
        P(None, None, "narrow"),
        P(None, "narrow"),
        P("narrow", None),
        P(),
        P(),
        P(),
        P(None, "narrow"),
        P(),
        P("narrow", None),
        P(),
        P("wide", "narrow", None),
    )
    out_specs = (
        P("wide", "narrow", None),
        P("wide", "narrow", None),
        P(),
        P(),
        P(),
        P(),
        P(None, None, "narrow"),
        P(None, "narrow"),
        P("narrow", None),
        P(),
        P(),
        P(),
        P(None, "narrow"),
        P("narrow"),
        P("narrow", None),
        P(),
    )
    return jax.shard_map(
        per_device, mesh=mesh, in_specs=in_specs, out_specs=out_specs, check_vma=False
    )
```

profile of v0, /device:TPU:0, one launch (start us, length us, event | category | flops | bytes accessed | tf_op | source)
XLA Modules:
  0.0 846.0 jit_solution(3704368714855647152)
XLA Ops:
  15.4 66.1 %all-gather.5.cloned.1.call-done = bf16[4,512,768]{1,2,0:T(8,128)(2,1)} async-done(((bf16[4,128,768]{1,2,0:T(8,128)(2,1)}), bf16[4,512,768]{1,2,0:T(8,128)(2,1)}) %all-gather.5.cloned.1.call-update) | async-done | bytes 3145744 | tf_op jit(solution)/shard_map/all_gather | solution.py:96
  81.5 4.0 fusion.5
  100.6 58.5 %reduce-scatter.13.cloned.1.call-done = bf16[128,3072]{1,0:T(8,128)(2,1)} async-done(((bf16[512,3072]{1,0:T(8,128)(2,1)}), bf16[128,3072]{1,0:T(8,128)(2,1)}) %reduce-scatter.13.cloned.1.call-update) | async-done | bytes 786448
  169.0 61.4 %all-gather.7.cloned.1.call-done = bf16[4,512,768]{1,2,0:T(8,128)(2,1)} async-done(((bf16[4,128,768]{1,2,0:T(8,128)(2,1)}), bf16[4,512,768]{1,2,0:T(8,128)(2,1)}) %all-gather.7.cloned.1.call-update) | async-done | bytes 3145744 | tf_op jit(solution)/shard_map/all_gather | solution.py:109
  230.4 7.5 multiply_convert_fusion.1
  237.9 55.6 %all-gather.9.cloned.1.call-done = bf16[4,512,768]{2,1,0:T(8,128)(2,1)} async-done(((bf16[4,128,768]{2,1,0:T(8,128)(2,1)}), bf16[4,512,768]{2,1,0:T(8,128)(2,1)}) %all-gather.9.cloned.1.call-update) | async-done | bytes 3145744 | tf_op jit(solution)/shard_map/all_gather | solution.py:121
  293.5 8.1 convert_reduce_fusion
  303.3 2.9 convolution_convert_fusion.1
  313.3 56.9 %reduce-scatter.17.cloned.1.call-done = bf16[128,3072]{1,0:T(8,128)(2,1)} async-done(((bf16[512,3072]{1,0:T(8,128)(2,1)}), bf16[128,3072]{1,0:T(8,128)(2,1)}) %reduce-scatter.17.cloned.1.call-update) | async-done | bytes 786448
  370.2 2.7 reshape.200
  379.5 4.8 convolution_convert_fusion.2
  389.5 53.4 %all-gather.11.cloned.1.call-done = bf16[4,512,768]{1,2,0:T(8,128)(2,1)} async-done(((bf16[4,128,768]{1,2,0:T(8,128)(2,1)}), bf16[4,512,768]{1,2,0:T(8,128)(2,1)}) %all-gather.11.cloned.1.call-update) | async-done | bytes 3145744 | tf_op jit(solution)/shard_map/all_gather | solution.py:134
  442.9 2.7 convolution_convert_fusion.3
  445.6 10.6 %multiply_reduce_fusion = (f32[4,3,512]{2,1,0:T(4,128)S(1)}, f32[4,3,512,512]{2,3,1,0:T(8,128)}) fusion(f32[4,3,512,512]{2,3,1,0:T(8,128)} %copy-done.2, f32[4,3,512]{2,1,0:T(4,128)S(1)} %copy-done.23, bf16[4,512,3,64]{1,3,2,0:T(8,128)(2,1)S(1)} %bitcast.173, bf16[4,512,3,64]{1,3,2,0:T(8,128)(2,1)S(1)} %bitcast.160), kind=kOutput, calls=%fused_computation.1 | convolution fusion | flops 415229952 | bytes 26787840 | tf_op jit(solution)/shard_map/clhe,cmhe->chlm/dot_general | solution.py:145
  458.9 6.9 multiply_convert_fusion
  469.6 3.2 convert_reduce_fusion.4
  472.8 3.0 bitcast_convert_fusion
  480.8 7.1 convolution_bitcast_fusion
  487.9 4.0 convolution_bitcast_fusion.1
  491.9 11.9 %reduce-scatter.15.cloned.1.call-done = bf16[128,3072]{1,0:T(8,128)(2,1)} async-done(((bf16[512,3072]{1,0:T(8,128)(2,1)}), bf16[128,3072]{1,0:T(8,128)(2,1)}) %reduce-scatter.15.cloned.1.call-update) | async-done | bytes 786448
  507.2 59.3 %reduce-scatter.19.cloned.1.call-done = bf16[128,3072]{1,0:T(8,128)(2,1)} async-done(((bf16[512,3072]{1,0:T(8,128)(2,1)}), bf16[128,3072]{1,0:T(8,128)(2,1)}) %reduce-scatter.19.cloned.1.call-update) | async-done | bytes 786448
  570.8 2.8 convert_reduce_fusion.1
  573.6 2.8 fusion.19
  576.5 3.5 convert_reduce_fusion.7
  582.2 4.0 convolution_bitcast_fusion.2
  586.3 5.3 fusion.23
  592.4 14.2 %all-reduce.1 = (f32[2,192]{1,0:T(2,128)}, f32[768]{0:T(1024)}) all-reduce(f32[2,192]{1,0:T(2,128)S(1)} %pad_maximum_fusion.6, f32[768]{0:T(1024)S(1)} %copy-done.57), channel_id=1, replica_groups=mesh['wide'=8,'narrow'=4] {'wide'}, use_global_device_ids=true, to_apply=%region_29.30 | all-reduce | flops 1152 | bytes 9216 | tf_op jit(solution)/shard_map/psum | solution.py:209
  608.0 41.0 %all-reduce = (f32[2,768]{1,0:T(2,128)}, f32[768]{0:T(1024)}, f32[768]{0:T(1024)}, f32[768]{0:T(1024)}, f32[768]{0:T(1024)}, /*index=5*/f32[768]{0:T(1024)}, f32[768]{0:T(1024)}) all-reduce(f32[2,768]{1,0:T(2,128)S(1)} %pad_maximum_fusion.4, f32[768]{0:T(1024)S(1)} %copy-done.49, ...), channel_id=1, replica_groups=mesh['wide'=8,'narrow'=4] {'wide','narrow'}, use_global_device_ids=true, to_apply=%region_21.22 | all-reduce | flops 6144 | bytes 49152 | tf_op jit(solution)/shard_map/psum | solution.py:196
  650.5 64.2 %all-reduce.6.cloned.1.call-done = f32[2,256,768]{1,2,0:T(8,128)} async-done(((f32[2,256,768]{1,2,0:T(8,128)}), f32[2,256,768]{1,2,0:T(8,128)}) %all-reduce.6.cloned.1.call-update) | async-done | bytes 1572880 | tf_op jit(solution)/shard_map/psum | solution.py:196
  714.7 3.0 copy.77
  717.7 113.3 %all-reduce.8.cloned.1.call-done = (f32[768,3,192]{0,2,1:T(8,128)}, f32[192,768]{1,0:T(8,128)}, f32[768,768]{1,0:T(8,128)}, f32[768,768]{1,0:T(8,128)}) async-done(((f32[768,3,192]{0,2,1:T(8,128)}, f32[192,768]{1,0:T(8,128)}, f32[768,768]{1,0:T(8,128)}, f32[768,768]{1,0:T(8,128)}), (f32[768,3,192]{0,2,1:T(8,128)}, f32[192,768]{1,0:T(8,128)}, f32[768,768]{1,0:T(8,128)}, ...) | async-done | bytes 7077904 | tf_op jit(solution)/shard_map/psum | solution.py:209
  831.0 2.9 copy.116
  (228 shorter events, 83.1 us)
Async XLA Ops:
  7.2 223.2 %copy-start = (bf16[768,768]{1,0:T(8,128)(2,1)S(1)}, bf16[768,768]{1,0:T(8,128)(2,1)}, u32[]{:S(2)}) copy-start(bf16[768,768]{1,0:T(8,128)(2,1)} %param.29) | copy-start | bytes 3538948
  7.2 74.3 %all-gather.5.cloned.1.call-start = ((), (), s32[]{:S(2)}) async-start(), calls=%async_computation.4 | async-start | bytes 3932160 | tf_op jit(solution)/shard_map/all_gather | solution.py:96
  12.3 69.2 %copy-start.64 = (bf16[768,3,192]{0,2,1:T(8,128)(2,1)S(1)}, bf16[768,3,192]{0,2,1:T(8,128)(2,1)}, u32[]{:S(2)}) copy-start(bf16[768,3,192]{0,2,1:T(8,128)(2,1)} %param.23) | copy-start | bytes 2654212
  15.2 143.9 %reduce-scatter.13.cloned.1.call-start = ((), (), s32[]{:S(2)}) async-start(), calls=%async_computation.9 | async-start | bytes 3932160
  100.4 62.1 %copy-start.58 = (f32[768]{0:T(1024)S(1)}, f32[768]{0:T(1024)}, u32[]{:S(2)}) copy-start(f32[768]{0:T(1024)} %param.26) | copy-start | bytes 9220
  100.4 130.0 %all-gather.7.cloned.1.call-start = ((), (), s32[]{:S(2)}) async-start(), calls=%async_computation.5 | async-start | bytes 3932160 | tf_op jit(solution)/shard_map/all_gather | solution.py:109
  167.0 126.5 %all-gather.9.cloned.1.call-start = ((), (), s32[]{:S(2)}) async-start(), calls=%async_computation.6 | async-start | bytes 3932160 | tf_op jit(solution)/shard_map/all_gather | solution.py:121
  167.5 202.7 %reduce-scatter.17.cloned.1.call-start = ((), (), s32[]{:S(2)}) async-start(), calls=%async_computation.11 | async-start | bytes 3932160
  311.0 131.9 %all-gather.11.cloned.1.call-start = ((), (), s32[]{:S(2)}) async-start(), calls=%async_computation.7 | async-start | bytes 3932160 | tf_op jit(solution)/shard_map/all_gather | solution.py:134
  379.5 124.4 %reduce-scatter.15.cloned.1.call-start = ((), (), s32[]{:S(2)}) async-start(), calls=%async_computation.10 | async-start | bytes 3932160
  389.2 53.7 %copy-start.21 = (bf16[192,768]{1,0:T(8,128)(2,1)S(1)}, bf16[192,768]{1,0:T(8,128)(2,1)}, u32[]{:S(2)}) copy-start(bf16[192,768]{1,0:T(8,128)(2,1)} %param.25) | copy-start | bytes 884740
  389.3 56.3 %copy-start.23 = (f32[4,3,512]{2,1,0:T(4,128)S(1)}, f32[4,3,512]{2,1,0:T(4,128)}, u32[]{:S(2)}) copy-start(f32[4,3,512]{2,1,0:T(4,128)} %copy-done.22) | copy-start | bytes 73732
  389.3 177.2 %reduce-scatter.19.cloned.1.call-start = ((), (), s32[]{:S(2)}) async-start(), calls=%async_computation.12 | async-start | bytes 3932160
  445.6 10.7 %slice-start = ((s8[12582912]{0:T(1024)(128)(4,1)}), s8[4194304]{0:T(1024)(128)(4,1)S(1)}, s32[]{:S(2)}) async-start(s8[12582912]{0:T(1024)(128)(4,1)} %bitcast.157), calls=%async_computation.14 | async-start | bytes 8388608
  445.6 12.0 %slice-start.1 = ((s8[12582912]{0:T(1024)(128)(4,1)}), s8[4194304]{0:T(1024)(128)(4,1)S(1)}, s32[]{:S(2)}) async-start(s8[12582912]{0:T(1024)(128)(4,1)} %bitcast.157), calls=%async_computation.15 | async-start | bytes 8388608
  445.6 13.3 %slice-start.2 = ((s8[12582912]{0:T(1024)(128)(4,1)}), s8[4194304]{0:T(1024)(128)(4,1)S(1)}, s32[]{:S(2)}) async-start(s8[12582912]{0:T(1024)(128)(4,1)} %bitcast.157), calls=%async_computation.16 | async-start | bytes 8388608
  480.6 234.1 %all-reduce.6.cloned.1.call-start = ((), (), s32[]{:S(2)}) async-start(), calls=%async_computation.8 | async-start | bytes 3145728 | tf_op jit(solution)/shard_map/psum | solution.py:196
  480.8 7.1 copy-start.63
  480.8 7.1 copy-start.68
  582.1 248.9 %all-reduce.8.cloned.1.call-start = ((), (), s32[]{:S(2)}) async-start(), calls=%async_computation.13 | async-start | bytes 14155776 | tf_op jit(solution)/shard_map/psum | solution.py:209
  591.6 15.1 %copy-start.39 = (f32[4,768]{1,0:T(4,128)S(1)}, f32[4,768]{1,0:T(4,128)}, u32[]{:S(2)}) copy-start(f32[4,768]{1,0:T(4,128)} %get-tuple-element.77) | copy-start | bytes 36868
  591.6 15.1 %copy-start.62 = (pred[4]{0:T(512)(128)(4,1)S(1)}, pred[4]{0:T(512)(128)(4,1)}, u32[]{:S(2)}) copy-start(pred[4]{0:T(512)(128)(4,1)} %copy-done.60) | copy-start | bytes 16
  591.6 15.2 %copy-start.13 = (bf16[4,128,768]{1,2,0:T(8,128)(2,1)S(1)}, bf16[4,128,768]{1,2,0:T(8,128)(2,1)}, u32[]{:S(2)}) copy-start(bf16[4,128,768]{1,2,0:T(8,128)(2,1)} %get-tuple-element.84) | copy-start | bytes 2359300
  591.6 16.4 %copy-start.46 = (f32[768]{0:T(1024)S(1)}, f32[768]{0:T(1024)}, u32[]{:S(2)}) copy-start(f32[768]{0:T(1024)} %get-tuple-element.54) | copy-start | bytes 9220
  591.6 16.4 %copy-start.47 = (f32[768]{0:T(1024)S(1)}, f32[768]{0:T(1024)}, u32[]{:S(2)}) copy-start(f32[768]{0:T(1024)} %get-tuple-element.50) | copy-start | bytes 9220
  591.6 16.4 %copy-start.48 = (f32[768]{0:T(1024)S(1)}, f32[768]{0:T(1024)}, u32[]{:S(2)}) copy-start(f32[768]{0:T(1024)} %get-tuple-element.56) | copy-start | bytes 9220
  591.6 16.4 %copy-start.49 = (f32[768]{0:T(1024)S(1)}, f32[768]{0:T(1024)}, u32[]{:S(2)}) copy-start(f32[768]{0:T(1024)} %get-tuple-element.52) | copy-start | bytes 9220
  591.7 16.4 %copy-start.50 = (f32[768]{0:T(1024)S(1)}, f32[768]{0:T(1024)}, u32[]{:S(2)}) copy-start(f32[768]{0:T(1024)} %get-tuple-element.85) | copy-start | bytes 9220
  591.7 16.4 %copy-start.51 = (f32[768]{0:T(1024)S(1)}, f32[768]{0:T(1024)}, u32[]{:S(2)}) copy-start(f32[768]{0:T(1024)} %get-tuple-element.75) | copy-start | bytes 9220
  591.7 57.3 %copy-start.25 = (bf16[4,128,768]{1,2,0:T(8,128)(2,1)S(1)}, bf16[4,128,768]{1,2,0:T(8,128)(2,1)}, u32[]{:S(2)}) copy-start(bf16[4,128,768]{1,2,0:T(8,128)(2,1)} %copy-done.24) | copy-start | bytes 2359300
  591.7 57.3 %copy-start.32 = (bf16[256,768]{1,0:T(8,128)(2,1)S(1)}, bf16[256,768]{1,0:T(8,128)(2,1)}, u32[]{:S(2)}) copy-start(bf16[256,768]{1,0:T(8,128)(2,1)} %copy-done.31) | copy-start | bytes 1179652
  591.7 57.3 %copy-start.34 = (bf16[256,768]{1,0:T(8,128)(2,1)S(1)}, bf16[256,768]{1,0:T(8,128)(2,1)}, u32[]{:S(2)}) copy-start(bf16[256,768]{1,0:T(8,128)(2,1)} %copy-done.33) | copy-start | bytes 1179652
  (50 other events, 153.0 us)
Sparse Core Ops, SparseCore 0:
  15.3 66.1 all-gather.4
  100.5 58.5 reduce-scatter.12
  167.1 63.2 all-gather.6
  231.8 61.6 all-gather.8
  311.1 59.0 reduce-scatter.16
  379.6 63.2 all-gather.10
  445.2 58.5 reduce-scatter.14
  506.1 60.3 reduce-scatter.18
  582.2 132.4 all-reduce.5
  719.4 111.5 all-reduce.7
where the time goes:
time: 856 us; the launch traced here: 846 us
  waiting for transfers between devices  601 us (70%)
  matrix products  80.5 us (9%)
  local copies, waits for them, and re-layouts  62.2 us (7%)
  blocking collectives  55.2 us (6%)
  other arithmetic  29.9 us (3%)
  between operations  15.4 us (2%)
    unnamed x14, waiting for transfers between devices  187 us
    psum x1, waiting for transfers between devices, per_device(): lax.psum((qkv_weight_grad, qv_bias_grad, out_weight_grad, up_weight_grad,...  113 us
    all_gather x1, waiting for transfers between devices, per_device(): rows_one = lax.all_gather(normed_one, 'narrow', axis=1, tiled=True)  66.1 us
    psum x1, waiting for transfers between devices, per_device(): lax.psum((proj_weight_grad, proj_bias_grad, ln1_gain_grad, ln1_bias_grad,...  64.2 us
    all_gather x1, waiting for transfers between devices, per_device(): rows_two = lax.all_gather(normed_two, 'narrow', axis=1, tiled=True)  61.4 us
    unnamed x167, local copies, waits for them, and re-layouts  58.5 us
    all_gather x1, waiting for transfers between devices, per_device(): grad_all = lax.all_gather(cotangent, 'narrow', axis=1, tiled=True)  55.6 us
    all_gather x1, waiting for transfers between devices, per_device(): mid_all = lax.all_gather(mid_low, 'narrow', axis=1, tiled=True)  53.4 us
  transfers between devices with their start and end apart: 10, of which 10 were waited for; matrix products, arithmetic and copies ran while one was open for 10% of the time, Pallas kernels for 0%

commit v1 on v0

v1 whole, which is shorter than its diff:
```python
import functools

import jax
import jax.numpy as jnp
from jax import lax
from jax.experimental import pallas as pl
from jax.experimental.pallas import tpu as pltpu
from jax.sharding import PartitionSpec as P

HEAD_DIM = 64
SCALE = HEAD_DIM ** (-0.5)
EPS = 1e-06
F32 = jnp.float32
BF16 = jnp.bfloat16
NN = (((1,), (0,)), ((), ()))
NT = (((1,), (1,)), ((), ()))
TN = (((0,), (0,)), ((), ()))


def dot(a, b, dims):
    return lax.dot_general(a, b, dims, preferred_element_type=F32)


def row_stats(v):
    mean = jnp.mean(v, axis=-1, keepdims=True)
    cen = v - mean
    var = jnp.mean(cen * cen, axis=-1, keepdims=True)
    return cen, lax.rsqrt(var + EPS)


def norm_back(v, grad, gain):
    cen, r = row_stats(v)
    xhat = cen * r
    q = grad * gain
    mq = jnp.mean(q, axis=-1, keepdims=True)
    mqx = jnp.mean(q * xhat, axis=-1, keepdims=True)
    return r * (q - mq - xhat * mqx), xhat


def gelu_pair(u):
    phi = 0.5 * (1.0 + lax.erf(u * (2.0 ** -0.5)))
    dens = jnp.exp(-0.5 * u * u) * 0.3989422804014327
    return u * phi, phi + u * dens


def attn_fwd_kernel(kind, x, proj, pbias, g1, b1, wq, bq, wo, ob, g2, b2,
                    start, n1, qkv, mixed, lse, middle, n2):
    z = pl.program_id(0)
    nz = pl.num_programs(0)

    @pl.when(z == 0)
    def _():
        s = dot(x[...], proj[0], NN) + pbias[0]
        start[...] = s
        middle[...] = s + ob[...]
        cen, r = row_stats(s)
        n1[...] = (cen * r * g1[...] + b1[...]).astype(BF16)

    qkv[0] = (dot(wq[0], n1[...], NT) + bq[0]).astype(BF16)
    width = mixed.shape[1]
    for h in range(width // HEAD_DIM):
        lo = h * HEAD_DIM
        q_t = qkv[0, lo:lo + HEAD_DIM, :]
        k_t = qkv[0, width + lo:width + lo + HEAD_DIM, :]
        v_t = qkv[0, 2 * width + lo:2 * width + lo + HEAD_DIM, :]
        s = dot(k_t, q_t, TN) * SCALE
        top = jnp.max(s, axis=0, keepdims=True)
        e = jnp.exp(s - top)
        total = jnp.sum(e, axis=0, keepdims=True)
        p = (e * (1.0 / total)).astype(BF16)
        lse[0, h:h + 1, :] = top + jnp.log(total)
        mixed[0, lo:lo + HEAD_DIM, :] = dot(v_t, p, NN).astype(BF16)
    middle[...] += dot(mixed[0], wo[0], TN)

    @pl.when(z == nz - 1)
    def _():
        cen, r = row_stats(middle[...])
        n2[...] = (cen * r * g2[...] + b2[...]).astype(BF16)


def ffn_kernel(n2, g, middle, up, ub, down, db, g2,
               out, mid_grad, mid_low, dup, ddown, dub, sums, acc, dn2, n2t):
    z = pl.program_id(0)
    nz = pl.num_programs(0)

    @pl.when(z == 0)
    def _():
        acc[...] = middle[...] + db[...]
        dn2[...] = jnp.zeros_like(dn2)
        n2t[...] = n2[...].T

    u = dot(n2[...], up[0], NN) + ub[0]
    h, slope = gelu_pair(u)
    h = h.astype(BF16)
    acc[...] += dot(h, down[0], NN)
    ddown[0] = dot(h, g[...], TN).astype(BF16)
    pre = (dot(g[...], down[0], NT) * slope).astype(BF16)
    dub[0] = jnp.sum(pre.astype(F32), axis=0, keepdims=True)
    dup[0] = dot(n2t[...], pre, NN).astype(BF16)
    dn2[...] += dot(pre, up[0], NT)

    @pl.when(z == nz - 1)
    def _():
        out[...] = acc[...].astype(BF16)
        gf = g[...].astype(F32)
        d = dn2[...]
        back, xhat = norm_back(middle[...], d, g2[...])
        mg = gf + back
        mid_grad[...] = mg
        ml = mg.astype(BF16)
        mid_low[...] = ml
        sums[...] = jnp.concatenate([
            jnp.sum(d * xhat, axis=0, keepdims=True),
            jnp.sum(d, axis=0, keepdims=True),
            jnp.sum(ml.astype(F32), axis=0, keepdims=True),
            jnp.sum(gf, axis=0, keepdims=True),
        ], axis=0)


def attn_bwd_kernel(kind, mid_low, mid_grad, start, n1, x, proj, g1, wq, wo, qkv, mixed, lse,
                    dqkv_w, dout_w, dqv, tok_grad, dproj, sums, dn1, dqkv):
    z = pl.program_id(0)
    nz = pl.num_programs(0)

    @pl.when(z == 0)
    def _():
        dn1[...] = jnp.zeros_like(dn1)

    ml = mid_low[...]
    dout_w[0] = dot(mixed[0], ml, NN).astype(BF16)
    do_all = dot(wo[0], ml, NT).astype(BF16)
    width = mixed.shape[1]
    for h in range(width // HEAD_DIM):
        lo = h * HEAD_DIM
        q_t = qkv[0, lo:lo + HEAD_DIM, :]
        k_t = qkv[0, width + lo:width + lo + HEAD_DIM, :]
        v_t = qkv[0, 2 * width + lo:2 * width + lo + HEAD_DIM, :]
        do_t = do_all[lo:lo + HEAD_DIM, :]
        p = jnp.exp(dot(k_t, q_t, TN) * SCALE - lse[0, h:h + 1, :])
        dp = dot(v_t, do_t, TN)
        dsum = jnp.sum(p * dp, axis=0, keepdims=True)
        ds = (p * (dp - dsum)).astype(BF16)
        dqkv[lo:lo + HEAD_DIM, :] = (dot(k_t, ds, NN) * SCALE).astype(BF16)
        dqkv[width + lo:width + lo + HEAD_DIM, :] = (dot(q_t, ds, NT) * SCALE).astype(BF16)
        dqkv[2 * width + lo:2 * width + lo + HEAD_DIM, :] = dot(do_t, p.astype(BF16), NT).astype(BF16)
    dw = dqkv[...]
    dqv[0] = jnp.sum(dw.astype(F32), axis=1, keepdims=True)
    dqkv_w[0] = dot(dw, n1[...], NN).astype(BF16)
    dn1[...] += dot(dw, wq[0], TN)

    @pl.when(z == nz - 1)
    def _():
        d = dn1[...]
        back, xhat = norm_back(start[...], d, g1[...])
        sl = (mid_grad[...] + back).astype(BF16)
        tok_grad[...] = dot(sl, proj[0], NT).astype(tok_grad.dtype)
        dproj[...] = dot(x[...], sl, TN)
        sums[...] = jnp.concatenate([
            jnp.sum(sl.astype(F32), axis=0, keepdims=True),
            jnp.sum(d * xhat, axis=0, keepdims=True),
            jnp.sum(d, axis=0, keepdims=True),
            jnp.zeros_like(g1[...]),
        ], axis=0)


def whole(shape):
    return pl.BlockSpec(shape, lambda z, *_: (0,) * len(shape))


def part(shape):
    return pl.BlockSpec((1,) + shape, lambda z, *_: (z,) + (0,) * len(shape))


def by_kind(shape):
    return pl.BlockSpec((1,) + shape, lambda z, k: (k[0],) + (0,) * len(shape))


def sds(shape, dtype):
    return jax.ShapeDtypeStruct(shape, dtype)


PARAMS = pltpu.CompilerParams(dimension_semantics=("arbitrary",), vmem_limit_bytes=56 << 20)


def attn_fwd(kind, x, proj, pbias, g1, b1, wq, bq, wo, ob, g2, b2):
    nz, qw, d = wq.shape
    hw = wo.shape[1]
    seq, feat = x.shape
    row = (1, d)
    return pl.pallas_call(
        attn_fwd_kernel,
        grid_spec=pltpu.PrefetchScalarGridSpec(
            num_scalar_prefetch=1, grid=(nz,),
            in_specs=[whole((seq, feat)), by_kind((feat, d)), by_kind(row), whole(row), whole(row),
                      part((qw, d)), part((qw, 1)), part((hw, d)), whole(row), whole(row), whole(row)],
            out_specs=[whole((seq, d)), whole((seq, d)), part((qw, seq)), part((hw, seq)),
                       part((8, seq)), whole((seq, d)), whole((seq, d))]),
        out_shape=[sds((seq, d), F32), sds((seq, d), BF16), sds((nz, qw, seq), BF16),
                   sds((nz, hw, seq), BF16), sds((nz, 8, seq), F32), sds((seq, d), F32),
                   sds((seq, d), BF16)],
        compiler_params=PARAMS, name="attn_fwd",
    )(kind, x, proj, pbias, g1, b1, wq, bq, wo, ob, g2, b2)


def ffn(n2, g, middle, up, ub, down, db, g2):
    nz, d, f = up.shape
    seq = n2.shape[0]
    row = (1, d)
    return pl.pallas_call(
        ffn_kernel,
        grid_spec=pltpu.PrefetchScalarGridSpec(
            num_scalar_prefetch=0, grid=(nz,),
            in_specs=[whole((seq, d)), whole((seq, d)), whole((seq, d)), part((d, f)), part((1, f)),
                      part((f, d)), whole(row), whole(row)],
            out_specs=[whole((seq, d)), whole((seq, d)), whole((seq, d)), part((d, f)), part((f, d)),
                       part((1, f)), whole((4, d))],
            scratch_shapes=[pltpu.VMEM((seq, d), F32), pltpu.VMEM((seq, d), F32),
                            pltpu.VMEM((d, seq), BF16)]),
        out_shape=[sds((seq, d), BF16), sds((seq, d), F32), sds((seq, d), BF16), sds((nz, d, f), BF16),
                   sds((nz, f, d), BF16), sds((nz, 1, f), F32), sds((4, d), F32)],
        compiler_params=PARAMS, name="ffn",
    )(n2, g, middle, up, ub, down, db, g2)


def attn_bwd(kind, mid_low, mid_grad, start, n1, x, proj, g1, wq, wo, qkv, mixed, lse):
    nz, qw, d = wq.shape
    hw = wo.shape[1]
    seq, feat = x.shape
    row = (1, d)
    return pl.pallas_call(
        attn_bwd_kernel,
        grid_spec=pltpu.PrefetchScalarGridSpec(
            num_scalar_prefetch=1, grid=(nz,),
            in_specs=[whole((seq, d)), whole((seq, d)), whole((seq, d)), whole((seq, d)),
                      whole((seq, feat)), by_kind((feat, d)), whole(row), part((qw, d)), part((hw, d)),
                      part((qw, seq)), part((hw, seq)), part((8, seq))],
            out_specs=[part((qw, d)), part((hw, d)), part((qw, 1)), whole((seq, feat)),
                       whole((feat, d)), whole((4, d))],
            scratch_shapes=[pltpu.VMEM((seq, d), F32), pltpu.VMEM((qw, seq), BF16)]),
        out_shape=[sds((nz, qw, d), BF16), sds((nz, hw, d), BF16), sds((nz, qw, 1), F32),
                   sds((seq, feat), BF16), sds((feat, d), F32), sds((4, d), F32)],
        compiler_params=PARAMS, name="attn_bwd",
    )(kind, mid_low, mid_grad, start, n1, x, proj, g1, wq, wo, qkv, mixed, lse)


def per_device(nw, nz, tokens, kind, proj_weight, proj_bias, ln1_gain, ln1_bias, qkv_weight, qv_bias,
               out_weight, out_bias, ln2_gain, ln2_bias, up_weight, up_bias, down_weight, down_bias,
               cotangent):
    me_w = lax.axis_index("wide")
    me_z = lax.axis_index("narrow")
    d = up_weight.shape[0]
    hw = out_weight.shape[0]

    def gather(shard):
        rows = shard.shape[0]
        mine = lax.dynamic_slice_in_dim(shard, me_w * (rows // nw), rows // nw, 0)
        full = lax.all_gather(mine, ("narrow", "wide"), axis=0, tiled=True)
        return full.reshape((nz, rows) + shard.shape[1:])

    def reduce(grad):
        rows = grad.shape[1]
        flat = grad.reshape((nz * rows,) + grad.shape[2:])
        mine = lax.psum_scatter(flat, ("narrow", "wide"), scatter_dimension=0, tiled=True)
        return lax.all_gather(mine, "wide", axis=0, tiled=True).astype(F32)

    def to_clip(v):
        return lax.all_to_all(v, "narrow", 0, 1, tiled=True)[0]

    def to_rows(v):
        return lax.all_to_all(v[None], "narrow", 1, 0, tiled=True)

    x = to_clip(tokens)
    wq = gather(jnp.transpose(qkv_weight, (1, 2, 0)).reshape(3 * hw, d))
    wo = gather(out_weight)
    up = gather(up_weight)
    down = gather(down_weight)
    g = to_clip(cotangent)
    zero_row = jnp.zeros_like(qv_bias[0])
    bias_three = jnp.concatenate([qv_bias[0], zero_row, qv_bias[1]])
    bq = lax.all_gather(bias_three, "narrow", axis=0)[:, :, None]
    ub = up_bias.reshape(nz, 1, d)
    my_kind = lax.dynamic_slice_in_dim(kind, me_z, 1, 0)
    my_kind = jnp.where(my_kind == 1, 1, 0).astype(jnp.int32)
    r = lambda v: v.reshape(1, d)

    start, n1, qkv, mixed, lse, middle, n2 = attn_fwd(
        my_kind, x, proj_weight, proj_bias[:, None, :], r(ln1_gain), r(ln1_bias), wq, bq, wo,
        r(out_bias), r(ln2_gain), r(ln2_bias))
    out, mid_grad, mid_low, dup, ddown, dub, sums2 = ffn(
        n2, g, middle, up, ub, down, r(down_bias), r(ln2_gain))
    dqkv_w, dout_w, dqv, tok_grad, dproj, sums1 = attn_bwd(
        my_kind, mid_low, mid_grad, start, n1, x, proj_weight, r(ln1_gain), wq, wo, qkv, mixed, lse)

    output = to_rows(out)
    tokens_grad = to_rows(tok_grad).astype(F32)
    dup_s = reduce(dup)
    ddown_s = reduce(ddown)
    dqkv_s = reduce(dqkv_w)
    dout_s = reduce(dout_w)
    is_patch = my_kind[0] == 1
    proj_pair = jnp.stack([jnp.where(is_patch, 0.0, dproj), jnp.where(is_patch, dproj, 0.0)])
    bias_pair = jnp.stack([jnp.where(is_patch, 0.0, sums1[0]), jnp.where(is_patch, sums1[0], 0.0)])
    dqv_cols = dqv.reshape(nz, 3, hw)
    small = jnp.concatenate([
        bias_pair, sums1[1:3], sums2, dub.reshape(nz, d),
        dqv_cols[:, 0].reshape(1, -1), dqv_cols[:, 2].reshape(1, -1)], axis=0)
    proj_sum = lax.psum(proj_pair.astype(BF16), ("wide", "narrow")).astype(F32)
    small = lax.psum(small, ("wide", "narrow"))
    up_b = lax.dynamic_index_in_dim(small, 8 + me_z, 0, keepdims=False)
    qv = lax.dynamic_slice_in_dim(small[8 + nz:10 + nz], me_z * hw, hw, 1)
    qkv_sum = jnp.transpose(dqkv_s.reshape(3, hw, d), (2, 0, 1))
    return (output, tokens_grad, proj_sum, small[0:2], small[2], small[3], qkv_sum, qv, dout_s,
            small[6], small[4], small[5], dup_s, up_b, ddown_s, small[7])


def solution(mesh):
    in_specs = (
        P("wide", "narrow", None), P("wide"), P(), P(), P(), P(), P(None, None, "narrow"),
        P(None, "narrow"), P("narrow", None), P(), P(), P(), P(None, "narrow"), P(),
        P("narrow", None), P(), P("wide", "narrow", None),
    )
    out_specs = (
        P("wide", "narrow", None), P("wide", "narrow", None), P(), P(), P(), P(),
        P(None, None, "narrow"), P(None, "narrow"), P("narrow", None), P(), P(), P(),
        P(None, "narrow"), P("narrow"), P("narrow", None), P(),
    )
    body = functools.partial(per_device, mesh.shape["wide"], mesh.shape["narrow"])
    return jax.shard_map(
        body, mesh=mesh, in_specs=in_specs, out_specs=out_specs, check_vma=False
    )
```

time: 856 us -> 918 us (1.072)
  matrix products: 80.5 us -> 0 us
  waiting for transfers between devices: 601 us -> 679 us
  Pallas kernels: 0 us -> 64.7 us
  blocking collectives: 55.2 us -> 104 us
  local copies, waits for them, and re-layouts: 62.2 us -> 21.7 us
  starting transfers between devices: 1.41 us -> 11.5 us
    reduce_scatter x0 -> x4, waiting for transfers between devices: none -> 377 us  [reduce(): lax.psum_scatter(flat, ('narrow', 'wide'), scatter_dimension=0, tiled=True)]
    unnamed x14 -> x11, waiting for transfers between devices: 187 us -> 2.02 us
    psum x2 -> x1, waiting for transfers between devices: 177 us -> 84.5 us  [per_device(): proj_sum = lax.psum(proj_pair.astype(BF16), ('wide', 'narrow')).astype(F32)]
    dot_general x21 -> x0, matrix products: 80.5 us -> none  [the longest x1 10.6 us: per_device(): jnp.einsum('clhe,cmhe->chlm', mixed_grad, heads_back[2], preferred_elemen...]
    pallas_call x0 -> x3, Pallas kernels: none -> 64.7 us  [the longest x1 24.2 us: attn_bwd(): pl.pallas_call(attn_bwd_kernel, grid_spec=pltpu.PrefetchScalarGridSpec(nu...]
    unnamed x167 -> x48, local copies, waits for them, and re-layouts: 58.5 us -> 5.78 us
    unnamed x0 -> x1, blocking collectives: none -> 27.5 us
    all_gather x4 -> x6, waiting for transfers between devices: 237 us -> 215 us  [the longest x4 180 us: gather(): full = lax.all_gather(mine, ('narrow', 'wide'), axis=0, tiled=True)]
  transfers between devices with their start and end apart: 10 -> 14, of which waited for: 10 -> 11; matrix products, arithmetic and copies ran while one was open for 10% -> 4% of each run, Pallas kernels for 0% -> 5%
where the time goes in v1:
time: 918 us; the launch traced here: 917 us
  waiting for transfers between devices  679 us (74%)
  blocking collectives  104 us (11%)
  Pallas kernels  64.7 us (7%)
  local copies, waits for them, and re-layouts  21.7 us (2%)
  other arithmetic  20.8 us (2%)
  between operations  15.6 us (2%)
  starting transfers between devices  11.5 us (1%)
    reduce_scatter x4, waiting for transfers between devices, reduce(): lax.psum_scatter(flat, ('narrow', 'wide'), scatter_dimension=0, tiled=True)  377 us
    all_gather x4, waiting for transfers between devices, gather(): full = lax.all_gather(mine, ('narrow', 'wide'), axis=0, tiled=True)  180 us
    psum x1, waiting for transfers between devices, per_device(): proj_sum = lax.psum(proj_pair.astype(BF16), ('wide', 'narrow')).astype(F32)  84.5 us
    psum x1, blocking collectives, per_device(): small = lax.psum(small, ('wide', 'narrow'))  41 us
    all_gather x2, waiting for transfers between devices, reduce(): return lax.all_gather(mine, 'wide', axis=0, tiled=True).astype(F32)  35.5 us
    unnamed x1, blocking collectives  27.5 us
    pallas_call x1, Pallas kernels, attn_bwd(): pl.pallas_call(attn_bwd_kernel, grid_spec=pltpu.PrefetchScalarGridSpec(nu...  24.2 us
    pallas_call x1, Pallas kernels, ffn(): pl.pallas_call(ffn_kernel, grid_spec=pltpu.PrefetchScalarGridSpec(num_sca...  23.2 us
  transfers between devices with their start and end apart: 14, of which 11 were waited for; matrix products, arithmetic and copies ran while one was open for 4% of the time, Pallas kernels for 5%

profile of v1, /device:TPU:0, one launch (start us, length us, event | category | flops | bytes accessed | tf_op | source)
XLA Modules:
  0.0 917.1 jit_solution(6644181757504023140)
XLA Ops:
  7.2 1.5 constant_dynamic-slice_fusion.3
  8.8 1.6 constant_dynamic-slice_fusion.4
  11.2 1.6 constant_dynamic-slice_fusion.2
  12.9 15.7 %all_to_all.19 = bf16[4,128,256]{2,1,0:T(8,128)(2,1)} all-to-all(bf16[4,128,256]{2,1,0:T(8,128)(2,1)} %param.17), channel_id=1, replica_groups=mesh['wide'=8,'narrow'=4] {'narrow'}, dimensions={0} | all-to-all | bytes 524288 | tf_op jit(solution)/shard_map/all_to_all | solution.py:267
  28.6 3.6 all-to-all-start.1
  33.8 27.5 %all-reduce = f32[2304]{0:T(1024)S(1)} all-reduce(f32[2304]{0:T(1024)S(1)} %maximum_dynamic-update-slice_fusion), channel_id=2, replica_groups=mesh['wide'=8,'narrow'=4] {'narrow'}, use_global_device_ids=true, to_apply=%add | all-reduce | flops 2304 | bytes 18432
  61.3 2.0 broadcast_in_dim.38.bq
  68.6 3.3 all-gather.10.cloned.1.call-done
  72.0 62.4 %all-gather.8.cloned.1.call-done = bf16[2304,768]{1,0:T(8,128)(2,1)} async-done(((bf16[72,768]{1,0:T(8,128)(2,1)}), bf16[2304,768]{1,0:T(8,128)(2,1)}) %all-gather.8.cloned.1.call-update) | async-done | bytes 3538960 | tf_op jit(solution)/shard_map/all_gather | solution.py:257
  134.4 17.2 %attn_fwd.1 = (f32[512,768]{1,0:T(8,128)}, bf16[512,768]{1,0:T(8,128)(2,1)}, bf16[4,576,512]{2,1,0:T(8,128)(2,1)}, bf16[4,192,512]{2,1,0:T(8,128)(2,1)}, f32[4,8...) custom-call(s32[1]{0:T(128)S(6)} %select_n.55.kind, bf16[512,256]{1,0:T(8,128)(2,1)} %bitcast.54, ...), custom_call_target="tpu_custom_call" | custom-call | tf_op jit(solution)/shard_map/attn_fwd/pallas_call | solution.py:190
  151.6 48.7 %all-gather.14.cloned.1.call-done = bf16[3072,768]{1,0:T(8,128)(2,1)} async-done(((bf16[96,768]{1,0:T(8,128)(2,1)}), bf16[3072,768]{1,0:T(8,128)(2,1)}) %all-gather.14.cloned.1.call-update) | async-done | bytes 4718608 | tf_op jit(solution)/shard_map/all_gather | solution.py:257
  200.3 65.3 %all-gather.12.cloned.1.call-done = bf16[3072,768]{1,0:T(8,128)(2,1)} async-done(((bf16[96,768]{1,0:T(8,128)(2,1)}), bf16[3072,768]{1,0:T(8,128)(2,1)}) %all-gather.12.cloned.1.call-update) | async-done | bytes 4718608 | tf_op jit(solution)/shard_map/all_gather | solution.py:257
  265.6 23.2 %ffn.1 = (bf16[512,768]{1,0:T(8,128)(2,1)}, f32[512,768]{1,0:T(8,128)}, bf16[512,768]{1,0:T(8,128)(2,1)}, bf16[4,768,768]{2,1,0:T(8,128)(2,1)}, bf16[4,768,768]{...) custom-call(bf16[512,768]{1,0:T(8,128)(2,1)} %get-tuple-element.36.n2, bf16[512,768]{1,0:T(8,128)(2,1)} %bitcast.53, ...), custom_call_target="tpu_custom_call" | custom-call | tf_op jit(solution)/shard_map/ffn/pallas_call | solution.py:209
  289.6 24.2 %attn_bwd.1 = (bf16[4,576,768]{2,1,0:T(8,128)(2,1)}, bf16[4,192,768]{2,1,0:T(8,128)(2,1)}, f32[4,576,1]{2,1,0:T(8,128)}, bf16[512,256]{1,0:T(8,128)(2,1)}, f32[256,768]{1,0:T(8,128)}, /*index=5*/f32[4,768]{1,0:T(4,128)}) custom-call(s32[1]{0:T(128)S(6)} %select_n.55.kind, bf16[512,768]{1,0:T(8,128)(2,1)} %get-tuple-element.39.mid_low, ...), custom_call_target="tpu_custom_call" | custom-call | tf_op jit(solution)/shard_map/attn_bwd/pallas_call | solution.py:230
  317.6 77.4 %reduce-scatter.9.cloned.1.call-done = bf16[96,768]{1,0:T(8,128)(2,1)} async-done(((bf16[3072,768]{1,0:T(8,128)(2,1)}), bf16[96,768]{1,0:T(8,128)(2,1)}) %reduce-scatter.9.cloned.1.call-update) | async-done | bytes 147472 | tf_op jit(solution)/shard_map/reduce_scatter | solution.py:263
  396.0 2.2 reduce.20
  399.0 3.4 all-to-all-start.3
  402.7 104.2 %reduce-scatter.11.cloned.1.call-done = bf16[96,768]{1,0:T(8,128)(2,1)} async-done(((bf16[3072,768]{1,0:T(8,128)(2,1)}), bf16[96,768]{1,0:T(8,128)(2,1)}) %reduce-scatter.11.cloned.1.call-update) | async-done | bytes 147472 | tf_op jit(solution)/shard_map/reduce_scatter | solution.py:263
  508.1 5.4 reduce.19
  514.6 3.6 all-to-all-start.2
  519.1 41.0 %psum.15 = f32[14,768]{1,0:T(8,128)S(1)} all-reduce(f32[14,768]{1,0:T(8,128)S(1)} %concatenate.7), channel_id=1, replica_groups=mesh['wide'=8,'narrow'=4] {'wide','narrow'}, use_global_device_ids=true, to_apply=%region_1.2 | all-reduce | flops 10752 | bytes 86016 | tf_op jit(solution)/shard_map/psum | solution.py:308
  563.0 84.5 %all-reduce.3.cloned.1.call-done = bf16[2,256,768]{2,1,0:T(8,128)(2,1)} async-done(((bf16[2,256,768]{2,1,0:T(8,128)(2,1)}), bf16[2,256,768]{2,1,0:T(8,128)(2,1)}) %all-reduce.3.cloned.1.call-update) | async-done | bytes 786448 | tf_op jit(solution)/shard_map/psum | solution.py:307
  647.5 2.4 convert_element_type.22
  651.6 97.7 %reduce-scatter.7.cloned.1.call-done = bf16[24,768]{1,0:T(8,128)(2,1)} async-done(((bf16[768,768]{1,0:T(8,128)(2,1)}), bf16[24,768]{1,0:T(8,128)(2,1)}) %reduce-scatter.7.cloned.1.call-update) | async-done | bytes 36880 | tf_op jit(solution)/shard_map/reduce_scatter | solution.py:263
  749.3 9.4 %all_gather.37 = bf16[192,768]{1,0:T(8,128)(2,1)S(1)} all-gather(bf16[24,768]{1,0:T(8,128)(2,1)} %reduce-scatter.7.cloned.1.call-done), channel_id=1, replica_groups=mesh['wide'=8,'narrow'=4] {'wide'}, dimensions={0}, use_global_device_ids=true | all-gather | bytes 331776 | tf_op jit(solution)/shard_map/all_gather | solution.py:264
  759.6 97.6 %reduce-scatter.5.cloned.1.call-done = bf16[72,768]{1,0:T(8,128)(2,1)} async-done(((bf16[2304,768]{1,0:T(8,128)(2,1)}), bf16[72,768]{1,0:T(8,128)(2,1)}) %reduce-scatter.5.cloned.1.call-update) | async-done | bytes 110608 | tf_op jit(solution)/shard_map/reduce_scatter | solution.py:263
  857.2 10.7 %all_gather.36 = bf16[576,768]{1,0:T(8,128)(2,1)S(1)} all-gather(bf16[72,768]{1,0:T(8,128)(2,1)} %reduce-scatter.5.cloned.1.call-done), channel_id=1, replica_groups=mesh['wide'=8,'narrow'=4] {'wide'}, dimensions={0}, use_global_device_ids=true | all-gather | bytes 995328 | tf_op jit(solution)/shard_map/all_gather | solution.py:264
  867.9 1.3 convert_bitcast_fusion
  869.2 12.6 %all-gather.16.cloned.1.call-done = bf16[768,768]{1,0:T(8,128)(2,1)} async-done(((bf16[96,768]{1,0:T(8,128)(2,1)}), bf16[768,768]{1,0:T(8,128)(2,1)}) %all-gather.16.cloned.1.call-update) | async-done | bytes 1179664 | tf_op jit(solution)/shard_map/all_gather | solution.py:264
  881.9 2.9 convert_element_type.24
  884.8 22.9 %all-gather.18.cloned.1.call-done = bf16[768,768]{1,0:T(8,128)(2,1)} async-done(((bf16[96,768]{1,0:T(8,128)(2,1)}), bf16[768,768]{1,0:T(8,128)(2,1)}) %all-gather.18.cloned.1.call-update) | async-done | bytes 1179664 | tf_op jit(solution)/shard_map/all_gather | solution.py:264
  907.7 2.8 convert_element_type.25
  (101 shorter events, 21.5 us)
Async XLA Ops:
  7.2 64.8 %all-gather.10.cloned.1.call-start = ((), (), s32[]{:S(2)}) async-start(), calls=%async_computation.9 | async-start | bytes 1216512 | tf_op jit(solution)/shard_map/all_gather | solution.py:257
  8.8 125.6 %all-gather.8.cloned.1.call-start = ((), (), s32[]{:S(2)}) async-start(), calls=%async_computation.8 | async-start | bytes 3649536 | tf_op jit(solution)/shard_map/all_gather | solution.py:257
  10.4 21.9 %copy-start.18 = (u32[32]{0:T(128)S(1)}, u32[32]{0:T(128)}, u32[]{:S(2)}) copy-start(u32[32]{0:T(128)} %constant.48) | copy-start | bytes 388
  10.4 23.2 %copy-start.16 = (f32[2,192]{1,0:T(2,128)S(1)}, f32[2,192]{1,0:T(2,128)}, u32[]{:S(2)}) copy-start(f32[2,192]{1,0:T(2,128)} %param.24) | copy-start | bytes 4612
  10.4 189.9 %all-gather.14.cloned.1.call-start = ((), (), s32[]{:S(2)}) async-start(), calls=%async_computation.11 | async-start | bytes 4866048 | tf_op jit(solution)/shard_map/all_gather | solution.py:257
  11.1 254.4 %all-gather.12.cloned.1.call-start = ((), (), s32[]{:S(2)}) async-start(), calls=%async_computation.10 | async-start | bytes 4866048 | tf_op jit(solution)/shard_map/all_gather | solution.py:257
  12.8 50.5 %copy-start.10 = (f32[768]{0:T(1024)S(1)}, f32[768]{0:T(1024)}, u32[]{:S(2)}) copy-start(f32[768]{0:T(1024)} %param.21) | copy-start | bytes 9220
  12.8 51.0 %copy-start.11 = (f32[768]{0:T(1024)S(1)}, f32[768]{0:T(1024)}, u32[]{:S(2)}) copy-start(f32[768]{0:T(1024)} %param.27) | copy-start | bytes 9220
  12.8 51.6 %copy-start.9 = (f32[2,768]{1,0:T(2,128)S(1)}, f32[2,768]{1,0:T(2,128)}, u32[]{:S(2)}) copy-start(f32[2,768]{1,0:T(2,128)} %param.20) | copy-start | bytes 18436
  12.8 52.2 %copy-start.12 = (f32[768]{0:T(1024)S(1)}, f32[768]{0:T(1024)}, u32[]{:S(2)}) copy-start(f32[768]{0:T(1024)} %param.22) | copy-start | bytes 9220
  12.9 52.8 %copy-start.13 = (f32[768]{0:T(1024)S(1)}, f32[768]{0:T(1024)}, u32[]{:S(2)}) copy-start(f32[768]{0:T(1024)} %param.26) | copy-start | bytes 9220
  28.6 37.6 %copy-start.14 = (f32[768]{0:T(1024)S(1)}, f32[768]{0:T(1024)}, u32[]{:S(2)}) copy-start(f32[768]{0:T(1024)} %param.28) | copy-start | bytes 9220
  28.6 38.2 %copy-start.15 = (f32[768]{0:T(1024)S(1)}, f32[768]{0:T(1024)}, u32[]{:S(2)}) copy-start(f32[768]{0:T(1024)} %param.32) | copy-start | bytes 9220
  28.6 38.8 %copy-start.17 = (s32[4]{0:T(128)S(1)}, s32[4]{0:T(128)}, u32[]{:S(2)}) copy-start(s32[4]{0:T(128)} %param.18) | copy-start | bytes 52
  28.6 123.0 %all-to-all-start.1 = ((bf16[4,128,768]{2,1,0:T(8,128)(2,1)}), bf16[4,128,768]{2,1,0:T(8,128)(2,1)S(1)}, u32[]{:S(2)}, u32[]{:S(2)}) async-start(bf16[4,128,768]{2,1,0:T(8,128)(2,1)} %param.33), calls=%async_computation.1 | async-start | bytes 1572864 | tf_op jit(solution)/shard_map/all_to_all | solution.py:267
  32.2 362.8 %reduce-scatter.9.cloned.1.call-start = ((), (), s32[]{:S(2)}) async-start(), calls=%async_computation.15 | async-start | bytes 4866048 | tf_op jit(solution)/shard_map/reduce_scatter | solution.py:263
  151.6 114.0 %copy-start.2 = (bf16[4,128,768]{2,1,0:T(8,128)(2,1)}, bf16[4,128,768]{2,1,0:T(8,128)(2,1)S(1)}, u32[]{:S(2)}) copy-start(bf16[4,128,768]{2,1,0:T(8,128)(2,1)S(1)} %all-to-all-done.1) | copy-start | bytes 2359300
  288.8 218.0 %reduce-scatter.11.cloned.1.call-start = ((), (), s32[]{:S(2)}) async-start(), calls=%async_computation.17 | async-start | bytes 4866048 | tf_op jit(solution)/shard_map/reduce_scatter | solution.py:263
  289.4 358.1 %all-reduce.3.cloned.1.call-start = ((), (), s32[]{:S(2)}) async-start(), calls=%async_computation.12 | async-start | bytes 1572864 | tf_op jit(solution)/shard_map/psum | solution.py:307
  316.1 433.3 %reduce-scatter.7.cloned.1.call-start = ((), (), s32[]{:S(2)}) async-start(), calls=%async_computation.14 | async-start | bytes 1216512 | tf_op jit(solution)/shard_map/reduce_scatter | solution.py:263
  316.8 540.4 %reduce-scatter.5.cloned.1.call-start = ((), (), s32[]{:S(2)}) async-start(), calls=%async_computation.13 | async-start | bytes 3649536 | tf_op jit(solution)/shard_map/reduce_scatter | solution.py:263
  316.9 78.2 %copy-start.5 = (bf16[512,256]{1,0:T(8,128)(2,1)S(1)}, bf16[512,256]{1,0:T(8,128)(2,1)}, u32[]{:S(2)}) copy-start(bf16[512,256]{1,0:T(8,128)(2,1)} %get-tuple-element.46) | copy-start | bytes 786436
  317.6 189.3 %copy-start.4 = (bf16[512,768]{1,0:T(8,128)(2,1)S(1)}, bf16[512,768]{1,0:T(8,128)(2,1)}, u32[]{:S(2)}) copy-start(bf16[512,768]{1,0:T(8,128)(2,1)} %get-tuple-element.38) | copy-start | bytes 2359300
  317.6 564.3 %all-gather.16.cloned.1.call-start = ((), (), s32[]{:S(2)}) async-start(), calls=%async_computation.16 | async-start | bytes 1327104 | tf_op jit(solution)/shard_map/all_gather | solution.py:264
  399.0 115.6 %all-to-all-start.3 = ((bf16[4,2,16384]{2,1,0:T(2,128)(2,1)}), bf16[4,2,16384]{2,1,0:T(2,128)(2,1)S(1)}, u32[]{:S(2)}, u32[]{:S(2)}) async-start(bf16[4,2,16384]{2,1,0:T(2,128)(2,1)} %reshape.150), calls=%async_computation.3 | async-start | bytes 524288 | tf_op jit(solution)/shard_map/all_to_all | solution.py:270
  402.4 505.3 %all-gather.18.cloned.1.call-start = ((), (), s32[]{:S(2)}) async-start(), calls=%async_computation.18 | async-start | bytes 1327104 | tf_op jit(solution)/shard_map/all_gather | solution.py:264
  513.5 4.7 copy-start.3
  514.5 4.4 copy-start.8
  514.5 4.4 copy-start.6
  514.5 4.4 copy-start.7
  514.6 135.3 %all-to-all-start.2 = ((bf16[4,2,49152]{2,1,0:T(2,128)(2,1)}), bf16[4,2,49152]{2,1,0:T(2,128)(2,1)S(1)}, u32[]{:S(2)}, u32[]{:S(2)}) async-start(bf16[4,2,49152]{2,1,0:T(2,128)(2,1)} %reshape.148), calls=%async_computation.2 | async-start | bytes 1572864 | tf_op jit(solution)/shard_map/all_to_all | solution.py:270
  881.9 28.7 %copy-start.1 = (bf16[768,768]{1,0:T(8,128)(2,1)S(1)}, bf16[768,768]{1,0:T(8,128)(2,1)}, u32[]{:S(2)}) copy-start(bf16[768,768]{1,0:T(8,128)(2,1)} %param.31) | copy-start | bytes 3538948
  (1 other events, 3.3 us)
Sparse Core Ops, SparseCore 0:
  11.5 60.4 all-gather.9
  75.4 58.8 all-gather.7
  137.8 62.3 all-gather.13
  203.6 61.9 all-gather.11
  288.9 106.0 reduce-scatter.8
  400.4 106.4 reduce-scatter.10
  512.6 134.8 all-reduce.2
  653.2 96.1 reduce-scatter.6
  754.8 102.3 reduce-scatter.4
  858.9 22.9 all-gather.15
  883.8 23.9 all-gather.17
